TPU v7x, 32 devices: a whole 2x2x4 slice. The times are simulated.
32 devices in a mesh: expert: 8 (over z, x), mp: 4 (over y, core).
Axes of the slice: x: 2, y: 2, z: 4, core: 2. Of those that a mesh axis runs over, the one named last changes fastest.
Arguments:
- routes: int32 [1024, 8], P('expert'), may hold values from 0 to 15, all different within a row; in each aligned block of 128 rows (0 to 127, 128 to 255, ...) at most 96 rows name the same one
- routed_hidden: bfloat16 [1024, 8, 1024], P('expert', None, 'mp'), may hold values from -36 to 36
- down_proj: bfloat16 [16, 1024, 3584], P('expert', None, 'mp'), may hold values from -6 to 6
- merge_group: int32 [16], replicated, may hold values from 0 to 7, as said below
Outputs:
- merged: bfloat16 [8, 1024, 3584], P('expert', None, 'mp')
Inputs may be any that keep to these rules, and one draw needn't show every extreme that they name: `routes`: among the 128 tokens of one index of the expert axis (aligned blocks of rows) no expert is named more than 96 times, a bound that some block reaches. `merge_group`: every group holds 1 to 3 experts, and some group holds exactly 3.
All inputs are finite; a program needn't handle non-finite values.
Results may differ from a plain program's by a relative error of at most 0.0056.
Values may be sent and summed in bfloat16 or wider, within the bound.
A program may use at most 128 MiB of HBM per device.

v0:
```python
import jax
import jax.numpy as jnp
from jax import lax
from jax.sharding import PartitionSpec as P

GMAX = 3


damping = 0.1
epsilon = 1e-05


def slot_rank(labels, label_count):
    onehot = (labels[:, None] == jnp.arange(label_count, dtype=jnp.int32)[None, :]).astype(
        jnp.int32
    )
    return jnp.sum(onehot * (jnp.cumsum(onehot, axis=0) - 1), axis=1)


def member_table(merge_group, group_count):
    expert_total = merge_group.shape[0]
    position = slot_rank(merge_group, group_count)
    slot_table = jnp.full((group_count * GMAX,), -1, jnp.int32)
    slot_table = slot_table.at[merge_group * GMAX + position].set(
        jnp.arange(expert_total, dtype=jnp.int32)
    )
    return slot_table.reshape(group_count, GMAX).T


def select_members(pieces, members):
    local_count = pieces.shape[0]
    present = members >= 0
    chosen = jnp.maximum(members, 0)
    picked = pieces[chosen % local_count, chosen // local_count]
    return jnp.where(present[:, :, None, None], picked, jnp.zeros((), pieces.dtype))


def solve_group(gram_sum, partial_value):
    order_size = gram_sum.shape[0]
    ridge_term = damping * jnp.trace(gram_sum) / order_size + epsilon
    system = gram_sum + ridge_term * jnp.eye(order_size, dtype=jnp.float32)
    factor = jnp.linalg.cholesky(system)
    return jax.scipy.linalg.cho_solve((factor, True), partial_value)


def member_work(member_rows, member_weights):
    gram_sum = jnp.einsum(
        "rsf,rsg->fg", member_rows, member_rows, preferred_element_type=jnp.float32
    )
    projected = jnp.einsum(
        "rsf,rfd->rsd", member_rows, member_weights, preferred_element_type=jnp.float32
    ).astype(jnp.bfloat16)
    partial_value = jnp.einsum(
        "rsf,rsd->fd", member_rows, projected, preferred_element_type=jnp.float32
    )
    return (gram_sum, partial_value)


def on_device(routes, routed_hidden, down_proj, merge_group):
    expert_count = lax.axis_size("expert")
    local_count = down_proj.shape[0]
    expert_total = local_count * expert_count
    tok_count, top_count = routes.shape
    hidden_part = routed_hidden.shape[2]
    full_width = down_proj.shape[1]
    out_part = down_proj.shape[2]
    slot_cap = 3 * tok_count * top_count // (2 * expert_total)
    row_count = tok_count * top_count
    targets = routes.reshape(row_count)
    position = slot_rank(targets, expert_total)
    members = member_table(merge_group, expert_count)
    piece_rows = full_width // expert_count
    member_rank = slot_rank(merge_group, expert_count)
    layer_index = member_rank[targets]
    dest_device = merge_group[targets]
    layer_count = GMAX
    slot_index = (layer_index * expert_count + dest_device) * slot_cap + position
    source_row = jnp.full((layer_count * expert_count * slot_cap,), row_count, jnp.int32)
    source_row = source_row.at[slot_index].set(jnp.arange(row_count, dtype=jnp.int32))
    padded = jnp.concatenate(
        [
            routed_hidden.reshape(row_count, hidden_part),
            jnp.zeros((1, hidden_part), routed_hidden.dtype),
        ],
        axis=0,
    )
    outgoing = padded[source_row].reshape(layer_count, expert_count * slot_cap, hidden_part)
    arrived = lax.all_to_all(outgoing, "expert", split_axis=1, concat_axis=1, tiled=True)
    expert_rows = lax.all_gather(arrived, "mp", axis=2, tiled=True)
    weight_pieces = down_proj.reshape(local_count, expert_count, piece_rows, out_part)
    weights_all = lax.all_to_all(weight_pieces, "expert", split_axis=1, concat_axis=1, tiled=True)
    weights_mine = lax.all_to_all(
        select_members(weights_all, members), "expert", split_axis=1, concat_axis=1, tiled=True
    )
    member_weights = weights_mine.reshape(GMAX, full_width, out_part)
    gram_sum, partial_value = member_work(expert_rows, member_weights)
    merged = solve_group(gram_sum, partial_value)
    return merged.astype(jnp.bfloat16).reshape(1, full_width, out_part)


def solution(mesh):
    return jax.shard_map(
        on_device,
        mesh=mesh,
        in_specs=(P("expert", None), P("expert", None, "mp"), P("expert", None, "mp"), P()),
        out_specs=P("expert", None, "mp"),
        check_vma=False,
    )
```

profile of v0, /device:TPU:0, one launch (start us, length us, event | category | flops | bytes accessed | tf_op | source)
XLA Modules:
  0.0 599.6 jit_solution(4867844247891751614)
XLA Ops:
  7.3 1.9 fusion.138
  11.9 4.5 compare_select_fusion.5
  16.5 4.5 reduce-window.6
  21.5 4.5 compare_select_fusion.6
  26.0 11.1 %fusion.126 = s32[1024]{0:T(1024)S(1)} fusion(s32[1024]{0:T(1024)S(1)} %fusion.90, pred[1024]{0:T(1024)(128)(4,1)S(1)} %get-tuple-element.21, pred[1024]{0:T(1024)(128)(4,1)S(1)} %get-tuple-element.20, pred[1024]{0:T(1024)(128)(4,1)S(1)} %get-tuple-element.19, pred[1024]{0:T(1024)(128)(4,1)S(1)} %get-tuple-element.18, ...), kind=kLoop, calls=%fused_computation.259 | loop fusion | flops 22528 | bytes 25672 | tf_op jit(solution)/shard_map/add | solution.py:77
  37.1 4.3 scatter_custom_fusion
  42.6 6.9 %gather_fusion = bf16[2304,256]{1,0:T(8,128)(2,1)S(1)} fusion(bf16[1025,256]{1,0:T(8,128)(2,1)S(1)} %concatenate.68, s32[3072]{0:T(1024)S(1)} %pad_clamp_fusion), kind=kCustom, calls=%fused_computation | custom fusion | bytes 2368512 | tf_op jit(solution)/shard_map/gather | solution.py:87
  50.5 44.1 %all_to_all.15 = bf16[3,768,256]{2,0,1:T(4,128)(2,1)S(1)} all-to-all(bf16[3,768,256]{2,0,1:T(4,128)(2,1)S(1)} %copy.40), channel_id=1, replica_groups=mesh['expert'=8,'mp'=4] {'expert'}, dimensions={1} | all-to-all | bytes 2359296 | tf_op jit(solution)/shard_map/all_to_all | solution.py:88
  95.7 4.2 copy.44
  100.0 4.7 all-to-all-start.1
  105.9 79.8 %all-to-all-done.1 = bf16[2,8,128,896]{3,2,0,1:T(8,128)(2,1)} async-done(((bf16[2,8,128,896]{3,2,0,1:T(8,128)(2,1)}), bf16[2,8,128,896]{3,2,0,1:T(8,128)(2,1)}, u32[]{:S(2)}, u32[]{:S(2)}) %all-to-all-start.1) | async-done | bytes 3670048 | tf_op jit(solution)/shard_map/all_to_all | solution.py:91
  185.7 5.8 gather_fusion.1
  191.5 5.6 copy_select_fusion
  197.1 4.7 all-to-all-start.2
  201.8 10.7 %select_reduce_fusion = (f32[]{:T(128)}, f32[1024,1024]{1,0:T(8,128)}) fusion(bf16[3,768,1024]{2,1,0:T(8,128)(2,1)} %all-gather.2.cloned.1.call-done), kind=kOutput, calls=%fused_computation.12 | convolution fusion | flops 4834983936 | bytes 8912900 | tf_op jit(solution)/shard_map/rsf,rsg->fg/dot_general | solution.py:47
  212.5 5.6 copy.43
  218.7 4.4 fusion.1
  223.1 2.0 copy-done.1
  225.1 11.7 %cholesky.222 = f32[128,128]{1,0:T(8,128)S(1)} custom-call(f32[128,128]{1,0:T(8,128)S(1)} %cholesky.577), custom_call_target="Cholesky" | custom-call | tf_op jit(solution)/shard_map/jit(cholesky)/cholesky | solution.py:42
  236.9 9.8 %custom-call.66 = f32[1,128,128]{1,2,0:T(8,128)S(1)} custom-call(f32[1,128,128]{2,1,0:T(8,128)S(1)} %get-tuple-element.72), custom_call_target="InvertDiagBlocksLowerTriangular" | custom-call | tf_op jit(solution)/shard_map/jit(cholesky)/cholesky | solution.py:42
  246.7 2.5 cholesky.254
  249.2 2.3 constant_dynamic-update-slice_fusion.43
  251.6 1.5 convolution_subtract_fusion.10
  253.1 12.1 %cholesky.243 = f32[128,128]{1,0:T(8,128)S(1)} custom-call(f32[128,128]{1,0:T(8,128)S(1)} %cholesky.581), custom_call_target="Cholesky" | custom-call | tf_op jit(solution)/shard_map/jit(cholesky)/cholesky | solution.py:42
  265.9 9.8 %custom-call.67 = f32[1,128,128]{1,2,0:T(8,128)S(1)} custom-call(f32[1,128,128]{2,1,0:T(8,128)S(1)} %get-tuple-element.69), custom_call_target="InvertDiagBlocksLowerTriangular" | custom-call | tf_op jit(solution)/shard_map/jit(cholesky)/cholesky | solution.py:42
  276.9 2.1 convolution_subtract_fusion.11
  279.0 11.7 %cholesky.466 = f32[128,128]{1,0:T(8,128)S(1)} custom-call(f32[128,128]{1,0:T(8,128)S(1)} %cholesky.586), custom_call_target="Cholesky" | custom-call | tf_op jit(solution)/shard_map/jit(cholesky)/cholesky | solution.py:42
  291.4 9.8 %custom-call.68 = f32[1,128,128]{1,2,0:T(8,128)S(1)} custom-call(f32[1,128,128]{2,1,0:T(8,128)S(1)} %get-tuple-element.66), custom_call_target="InvertDiagBlocksLowerTriangular" | custom-call | tf_op jit(solution)/shard_map/jit(cholesky)/cholesky | solution.py:42
  302.4 2.3 convolution_subtract_fusion.12
  304.8 11.9 %cholesky.485 = f32[128,128]{1,0:T(8,128)S(1)} custom-call(f32[128,128]{1,0:T(8,128)S(1)} %cholesky.591), custom_call_target="Cholesky" | custom-call | tf_op jit(solution)/shard_map/jit(cholesky)/cholesky | solution.py:42
  317.3 9.8 %custom-call.69 = f32[1,128,128]{1,2,0:T(8,128)S(1)} custom-call(f32[1,128,128]{2,1,0:T(8,128)S(1)} %get-tuple-element.63), custom_call_target="InvertDiagBlocksLowerTriangular" | custom-call | tf_op jit(solution)/shard_map/jit(cholesky)/cholesky | solution.py:42
  328.2 2.3 convolution_subtract_fusion.13
  330.6 11.7 %cholesky.504 = f32[128,128]{1,0:T(8,128)S(1)} custom-call(f32[128,128]{1,0:T(8,128)S(1)} %cholesky.596), custom_call_target="Cholesky" | custom-call | tf_op jit(solution)/shard_map/jit(cholesky)/cholesky | solution.py:42
  342.9 10.0 %custom-call.70 = f32[1,128,128]{1,2,0:T(8,128)S(1)} custom-call(f32[1,128,128]{2,1,0:T(8,128)S(1)} %get-tuple-element.60), custom_call_target="InvertDiagBlocksLowerTriangular" | custom-call | tf_op jit(solution)/shard_map/jit(cholesky)/cholesky | solution.py:42
  354.0 2.3 convolution_subtract_fusion.14
  356.3 11.7 %cholesky.524 = f32[128,128]{1,0:T(8,128)S(1)} custom-call(f32[128,128]{1,0:T(8,128)S(1)} %cholesky.601), custom_call_target="Cholesky" | custom-call | tf_op jit(solution)/shard_map/jit(cholesky)/cholesky | solution.py:42
  368.6 9.8 %custom-call.71 = f32[1,128,128]{1,2,0:T(8,128)S(1)} custom-call(f32[1,128,128]{2,1,0:T(8,128)S(1)} %get-tuple-element.57), custom_call_target="InvertDiagBlocksLowerTriangular" | custom-call | tf_op jit(solution)/shard_map/jit(cholesky)/cholesky | solution.py:42
  379.4 2.0 convolution_subtract_fusion.15
  381.4 11.7 %cholesky.544 = f32[128,128]{1,0:T(8,128)S(1)} custom-call(f32[128,128]{1,0:T(8,128)S(1)} %cholesky.606), custom_call_target="Cholesky" | custom-call | tf_op jit(solution)/shard_map/jit(cholesky)/cholesky | solution.py:42
  393.8 10.1 %custom-call.72 = f32[1,128,128]{1,2,0:T(8,128)S(1)} custom-call(f32[1,128,128]{2,1,0:T(8,128)S(1)} %get-tuple-element.54), custom_call_target="InvertDiagBlocksLowerTriangular" | custom-call | tf_op jit(solution)/shard_map/jit(cholesky)/cholesky | solution.py:42
  404.8 1.8 convolution_subtract_fusion.16
  406.6 11.7 %cholesky.562 = f32[128,128]{1,0:T(8,128)S(1)} custom-call(f32[128,128]{1,0:T(8,128)S(1)} %convolution_subtract_fusion.16), custom_call_target="Cholesky" | custom-call | tf_op jit(solution)/shard_map/jit(cholesky)/cholesky | solution.py:42
  428.6 4.8 select_select_fusion
  433.5 23.0 %while.1 = (s32[]{:T(128)}, f32[1024,1024]{1,0:T(8,128)}, s32[8,2]{0,1:T(2,128)S(1)}, f32[8,128,128]{2,1,0:T(8,128)S(1)}, s32[]{:T(128)}) while((s32[]{:T(128)}, f32[1024,1024]{1,0:T(8,128)}, s32[8,2]{0,1:T(2,128)S(1)}, f32[8,128,128]{2,1,0:T(8,128)S(1)}, s32[]{:T(128)}) %tuple.99), condition=%wide.while_cond, body=%wide.while_body.sunk | while | flops 2 | bytes 131189 | solution.py:43
  434.1 2.3 bitcast_dynamic-update-slice_fusion.9
  437.0 2.3 bitcast_dynamic-update-slice_fusion.9
  439.8 2.3 bitcast_dynamic-update-slice_fusion.9
  442.7 2.3 bitcast_dynamic-update-slice_fusion.9
  445.6 2.3 bitcast_dynamic-update-slice_fusion.9
  448.5 2.3 bitcast_dynamic-update-slice_fusion.9
  451.4 2.3 bitcast_dynamic-update-slice_fusion.9
  454.3 2.2 bitcast_dynamic-update-slice_fusion.9
  456.5 78.8 %custom-call.73 = f32[8,128,128]{1,2,0:T(8,128)S(1)} custom-call(f32[8,128,128]{2,1,0:T(8,128)S(1)} %get-tuple-element.12), custom_call_target="InvertDiagBlocksLowerTriangular" | custom-call | tf_op jit(solution)/shard_map/jit(_cho_solve)/triangular_solve | solution.py:43
  535.3 5.7 copy.47
  540.9 17.1 %fusion.4 = f32[1024,896]{1,0:T(8,128)} fusion(bf16[3,768,1024]{2,1,0:T(8,128)(2,1)} %all-gather.2.cloned.1.call-done, bf16[3,1024,896]{2,1,0:T(8,128)(2,1)} %bitcast.231), kind=kOutput, calls=%fused_computation.18 | convolution fusion | flops 8457781248 | bytes 13893632 | tf_op jit(solution)/shard_map/rsf,rsd->fd/dot_general | solution.py:53
  558.0 1.8 constant_dynamic-update-slice_fusion.10
  559.8 1.6 convolution_subtract_fusion.9
  562.1 2.0 convolution_subtract_fusion.5
  568.5 1.6 convolution_subtract_fusion.8
  570.7 1.7 convolution_subtract_fusion.4
  573.0 2.1 convolution_subtract_fusion.1
  582.4 1.7 convolution_subtract_fusion.6
  584.8 1.8 convolution_subtract_fusion.2
  587.4 2.2 convolution_subtract_fusion
  (139 shorter events, 46.1 us)
Async XLA Ops:
  6.5 195.3 %all-gather.2.cloned.1.call-start = ((), (), s32[]{:S(2)}) async-start(), calls=%async_computation.3 | async-start | bytes 5898240 | tf_op jit(solution)/shard_map/all_gather | solution.py:89
  100.0 4.8 copy-start.3
  100.0 85.8 %all-to-all-start.1 = ((bf16[2,8,128,896]{3,2,0,1:T(8,128)(2,1)}), bf16[2,8,128,896]{3,2,0,1:T(8,128)(2,1)}, u32[]{:S(2)}, u32[]{:S(2)}) async-start(bf16[2,8,128,896]{3,2,0,1:T(8,128)(2,1)} %copy.44), calls=%async_computation.1 | async-start | bytes 7340032 | tf_op jit(solution)/shard_map/all_to_all | solution.py:91
  197.1 338.2 %all-to-all-start.2 = ((bf16[3,8,128,896]{3,2,0,1:T(8,128)(2,1)}), bf16[3,8,128,896]{3,2,0,1:T(8,128)(2,1)}, u32[]{:S(2)}, u32[]{:S(2)}) async-start(bf16[3,8,128,896]{3,2,0,1:T(8,128)(2,1)} %copy_select_fusion), calls=%async_computation.2 | async-start | bytes 11010048 | tf_op jit(solution)/shard_map/all_to_all | solution.py:92
  223.1 2.0 copy-start.1
  558.0 4.0 copy-start
  561.4 3.3 copy-start.2
  590.4 1.2 copy-start.4
Sparse Core Ops, SparseCore 0:
  95.9 37.0 all-gather.1
where the time goes:
time: 608 us; the launch traced here: 600 us
  other arithmetic  293 us (48%)
  matrix products  82.1 us (14%)
  waiting for transfers between devices  79.8 us (13%)
  local copies, waits for them, and re-layouts  70 us (12%)
  blocking collectives  44.1 us (7%)
  between operations  20.5 us (3%)
  starting transfers between devices  9.41 us (2%)
    another operation x30, other arithmetic, solve_group(): factor = jnp.linalg.cholesky(system)  172 us
    another operation x4, other arithmetic, solve_group(): return jax.scipy.linalg.cho_solve((factor, True), partial_value)  84.3 us
    all_to_all x1, waiting for transfers between devices, on_device(): lax.all_to_all(weight_pieces, 'expert', split_axis=1, concat_axis=1, tile...  79.8 us
    all_to_all x1, blocking collectives, on_device(): lax.all_to_all(outgoing, 'expert', split_axis=1, concat_axis=1, tiled=True)  44.1 us
    another operation x30, matrix products, solve_group(): return jax.scipy.linalg.cho_solve((factor, True), partial_value)  31.2 us
    another operation x28, local copies, waits for them, and re-layouts  23.1 us
    another operation x14, matrix products, solve_group(): factor = jnp.linalg.cholesky(system)  23.1 us
    dot_general x1, matrix products, member_work(): jnp.einsum('rsf,rsd->fd', member_rows, projected, preferred_element_type=...  17.1 us
  transfers between devices with their start and end apart: 3, of which 1 were waited for; matrix products, arithmetic and copies ran while one was open for 57% of the time, Pallas kernels for 0%

commit v1 on v0

v1 whole, which is shorter than its diff:
```python
import jax
import jax.numpy as jnp
from jax import lax
from jax.experimental import pallas as pl
from jax.experimental.pallas import tpu as pltpu
from jax.sharding import PartitionSpec as P

GMAX = 3
BLOCK = 128
PANEL = 8

damping = 0.1
epsilon = 1e-05
HIGHEST = lax.Precision.HIGHEST


def slot_rank(labels, label_count):
    count = labels.shape[0]
    onehot = labels[:, None] == jnp.arange(label_count, dtype=jnp.int32)[None, :]
    order = jnp.arange(count, dtype=jnp.int32)
    before = (order[None, :] < order[:, None]).astype(jnp.bfloat16)
    ahead = jnp.dot(before, onehot.astype(jnp.bfloat16), preferred_element_type=jnp.float32)
    return jnp.sum(jnp.where(onehot, ahead, 0.0), axis=1).astype(jnp.int32)


def invert_small(entry):
    size = len(entry)
    value = {(i, j): entry[i][j] for i in range(size) for j in range(i, size)}

    def get(i, j):
        return value[(min(i, j), max(i, j))]

    for k in range(0, size, 2):
        a, b, d = get(k, k), get(k, k + 1), get(k + 1, k + 1)
        scale = 1.0 / (a * d - b * b)
        a, b, d = a * scale, b * scale, d * scale
        others = [i for i in range(size) if i not in (k, k + 1)]
        scaled = {
            i: (get(i, k) * d - get(i, k + 1) * b, get(i, k + 1) * a - get(i, k) * b)
            for i in others
        }
        for i in others:
            for j in others:
                if i <= j:
                    value[(i, j)] = value[(i, j)] - (
                        scaled[i][0] * get(j, k) + scaled[i][1] * get(j, k + 1)
                    )
        for i in others:
            value[(min(i, k), max(i, k))] = scaled[i][0]
            value[(min(i, k + 1), max(i, k + 1))] = scaled[i][1]
        value[(k, k)], value[(k, k + 1)], value[(k + 1, k + 1)] = -d, b, -a
    return [[-get(i, j) for j in range(size)] for i in range(size)]


def tree_sum(terms):
    while len(terms) > 1:
        terms = [sum(terms[i : i + 2][1:], terms[i]) for i in range(0, len(terms), 2)]
    return terms[0]


def invert_tile(tile_ref):
    size = tile_ref.shape[0]
    full = (PANEL, size)
    lane = lax.broadcasted_iota(jnp.int32, full, 1)
    sub = lax.broadcasted_iota(jnp.int32, full, 0)
    panels = size // PANEL
    group = [tile_ref[g * PANEL : (g + 1) * PANEL, :] for g in range(panels)]
    for p in range(panels):
        first = p * PANEL
        columns = [jnp.broadcast_to(group[p][:, first + j : first + j + 1], full) for j in range(PANEL)]
        entry = [
            [jnp.broadcast_to(columns[j][i : i + 1, :], full) for j in range(PANEL)]
            for i in range(PANEL)
        ]
        inverse = invert_small(entry)
        own = [inverse[0][j] for j in range(PANEL)]
        for i in range(1, PANEL):
            own = [jnp.where(sub == i, inverse[i][j], own[j]) for j in range(PANEL)]
        row = [jnp.broadcast_to(group[p][j : j + 1, :], full) for j in range(PANEL)]
        scaled = tree_sum([own[j] * row[j] for j in range(PANEL)])
        for j in range(PANEL):
            scaled = jnp.where(lane == first + j, own[j], scaled)
        spread = [jnp.broadcast_to(scaled[j : j + 1, :], full) for j in range(PANEL)]
        pivots = (lane >= first) & (lane < first + PANEL)
        order = [(p + 1 + g) % panels for g in range(panels - 1)]
        for g in order:
            here = group[g]
            group[g] = jnp.where(pivots, 0.0, here) - tree_sum(
                [
                    jnp.broadcast_to(here[:, first + j : first + j + 1], full) * spread[j]
                    for j in range(PANEL)
                ]
            )
        group[p] = scaled
    for g in range(panels):
        tile_ref[g * PANEL : (g + 1) * PANEL, :] = group[g]


def inverse_kernel(a_ref, o_ref, s_ref, d_ref):
    size = a_ref.shape[0]
    o_ref[...] = a_ref[...]
    tiles = size // BLOCK

    def eliminate(step, carry):
        span = pl.ds(pl.multiple_of(step * BLOCK, BLOCK), BLOCK)
        d_ref[...] = o_ref[span, span]
        invert_tile(d_ref)
        inverse = d_ref[...]
        s_ref[...] = jnp.dot(
            inverse, o_ref[span, :], precision=HIGHEST, preferred_element_type=jnp.float32
        )
        s_ref[:, span] = inverse

        def update(tile, inner):
            here = pl.ds(pl.multiple_of(tile * BLOCK, BLOCK), BLOCK)
            column = o_ref[here, span]
            o_ref[here, span] = jnp.zeros((BLOCK, BLOCK), jnp.float32)
            o_ref[here, :] = o_ref[here, :] - jnp.dot(
                column, s_ref[...], precision=HIGHEST, preferred_element_type=jnp.float32
            )
            return inner

        lax.fori_loop(0, tiles, update, 0)
        o_ref[span, :] = s_ref[...]
        return carry

    lax.fori_loop(0, tiles, eliminate, 0)


def spd_inverse(system):
    size = system.shape[0]
    return pl.pallas_call(
        inverse_kernel,
        out_shape=jax.ShapeDtypeStruct(system.shape, jnp.float32),
        in_specs=[pl.BlockSpec(memory_space=pltpu.VMEM)],
        out_specs=pl.BlockSpec(memory_space=pltpu.VMEM),
        scratch_shapes=[
            pltpu.VMEM((BLOCK, size), jnp.float32),
            pltpu.VMEM((BLOCK, BLOCK), jnp.float32),
        ],
        compiler_params=pltpu.CompilerParams(vmem_limit_bytes=24 << 20),
        cost_estimate=pl.CostEstimate(
            flops=50 * size**3, bytes_accessed=8 * size * size, transcendentals=0
        ),
    )(system)


def on_device(routes, routed_hidden, down_proj, merge_group):
    expert_count = lax.axis_size("expert")
    local_count = down_proj.shape[0]
    expert_total = local_count * expert_count
    tok_count, top_count = routes.shape
    hidden_part = routed_hidden.shape[2]
    full_width = down_proj.shape[1]
    out_part = down_proj.shape[2]
    slot_cap = 3 * tok_count * top_count // (2 * expert_total)
    row_count = tok_count * top_count
    piece_rows = full_width // expert_count

    weight_pieces = down_proj.reshape(local_count, expert_count, piece_rows, out_part)
    weights_all = lax.all_to_all(weight_pieces, "expert", split_axis=1, concat_axis=1, tiled=True)

    experts = jnp.arange(expert_total, dtype=jnp.int32)
    member_rank = slot_rank(merge_group, expert_count)
    first_slot = (member_rank * expert_count + merge_group) * slot_cap
    targets = routes.reshape(row_count)
    position = slot_rank(targets, expert_total)
    slot_index = position + jnp.sum(
        jnp.where(targets[:, None] == experts[None, :], first_slot[None, :], 0), axis=1
    )
    slots = jnp.arange(GMAX * expert_count * slot_cap, dtype=jnp.int32)
    chosen = (slots[:, None] == slot_index[None, :]).astype(jnp.bfloat16)
    outgoing = jnp.dot(
        chosen,
        routed_hidden.reshape(row_count, hidden_part),
        preferred_element_type=jnp.float32,
    ).astype(jnp.bfloat16)
    outgoing = outgoing.reshape(GMAX, expert_count * slot_cap, hidden_part)
    arrived = lax.all_to_all(outgoing, "expert", split_axis=1, concat_axis=1, tiled=True)
    rows = lax.all_gather(arrived, "mp", axis=2, tiled=True)

    table = jnp.arange(GMAX * expert_count, dtype=jnp.int32)
    place = member_rank * expert_count + merge_group
    members = jnp.sum(jnp.where(table[:, None] == place[None, :], experts[None, :], 0), axis=1)
    picked = weights_all.reshape(expert_total, piece_rows, out_part)[
        (members % local_count) * expert_count + members // local_count
    ].reshape(GMAX, expert_count, piece_rows, out_part)
    weights_mine = lax.all_to_all(picked, "expert", split_axis=1, concat_axis=1, tiled=True)
    member_weights = weights_mine.reshape(GMAX, full_width, out_part)

    flat_rows = rows.reshape(-1, full_width)
    gram_sum = lax.dot_general(
        flat_rows, flat_rows, (((0,), (0,)), ((), ())), preferred_element_type=jnp.float32
    )
    ridge_term = damping * jnp.trace(gram_sum) / full_width + epsilon
    inverse = spd_inverse(gram_sum + ridge_term * jnp.eye(full_width, dtype=jnp.float32))

    projected = jnp.einsum(
        "rsf,rfd->rsd", rows, member_weights, preferred_element_type=jnp.float32
    ).astype(jnp.bfloat16)
    partial_value = lax.dot_general(
        flat_rows,
        projected.reshape(-1, out_part),
        (((0,), (0,)), ((), ())),
        preferred_element_type=jnp.float32,
    )
    merged = jnp.dot(
        inverse, partial_value, precision=HIGHEST, preferred_element_type=jnp.float32
    )
    return merged.astype(jnp.bfloat16).reshape(1, full_width, out_part)


def solution(mesh):
    return jax.shard_map(
        on_device,
        mesh=mesh,
        in_specs=(P("expert", None), P("expert", None, "mp"), P("expert", None, "mp"), P()),
        out_specs=P("expert", None, "mp"),
        check_vma=False,
    )
```

time: 608 us -> 332 us (0.55); the launches traced: 600 us -> 332 us
  other arithmetic: 293 us -> 3.42 us
  Pallas kernels: 0 us -> 79.4 us
  waiting for transfers between devices: 79.8 us -> 138 us
  blocking collectives: 44.1 us -> 0 us
  local copies, waits for them, and re-layouts: 70 us -> 32 us
  matrix products: 82.1 us -> 48.3 us
  starting transfers between devices: 9.41 us -> 16.7 us
  between operations: 20.5 us -> 14.1 us
    another operation x37 -> x0, other arithmetic: 261 us -> none  [the longest x30 172 us: solve_group(): factor = jnp.linalg.cholesky(system)]
    pallas_call x0 -> x1, Pallas kernels: none -> 79.4 us  [spd_inverse(): pl.pallas_call(inverse_kernel, out_shape=jax.ShapeDtypeStruct(system.shap...]
    all_to_all x1 -> x2, waiting for transfers between devices: 0.01 us -> 57.8 us  [the longest x1 32.7 us: on_device(): lax.all_to_all(outgoing, 'expert', split_axis=1, concat_axis=1, tiled=True)]
    another operation x44 -> x0, matrix products: 54.4 us -> none  [the longest x30 31.2 us: solve_group(): return jax.scipy.linalg.cho_solve((factor, True), partial_value)]
    all_to_all x1 -> x0, blocking collectives: 44.1 us -> none  [on_device(): lax.all_to_all(outgoing, 'expert', split_axis=1, concat_axis=1, tiled=True)]
    another operation x40 -> x0, local copies, waits for them, and re-layouts: 25.8 us -> none
    dot_general x2 -> x6, matrix products: 27.8 us -> 48.3 us  [the longest x1 17.3 us: on_device(): jnp.dot(inverse, partial_value, precision=HIGHEST, preferred_element_type...]
    gather x4 -> x1, local copies, waits for them, and re-layouts: 15.3 us -> 5.93 us  [on_device(): weights_all.reshape(expert_total, piece_rows, out_part)]
  transfers between devices with their start and end apart: 3 -> 4, of which waited for: 1 -> 3; matrix products, arithmetic and copies ran while one was open for 57% -> 10% of each run, Pallas kernels for 0% -> 24%
where the time goes in v1:
time: 332 us
  waiting for transfers between devices  138 us (42%)
  Pallas kernels  79.4 us (24%)
  matrix products  48.3 us (15%)
  local copies, waits for them, and re-layouts  32 us (10%)
  starting transfers between devices  16.7 us (5%)
  between operations  14.1 us (4%)
  other arithmetic  3.42 us (1%)
    all_to_all x1, waiting for transfers between devices, on_device(): lax.all_to_all(weight_pieces, 'expert', split_axis=1, concat_axis=1, tile...  80 us
    pallas_call x1, Pallas kernels, spd_inverse(): pl.pallas_call(inverse_kernel, out_shape=jax.ShapeDtypeStruct(system.shap...  79.4 us
    all_to_all x1, waiting for transfers between devices, on_device(): lax.all_to_all(outgoing, 'expert', split_axis=1, concat_axis=1, tiled=True)  32.7 us
    all_to_all x1, waiting for transfers between devices, on_device(): lax.all_to_all(picked, 'expert', split_axis=1, concat_axis=1, tiled=True)  25.1 us
    dot_general x1, matrix products, on_device(): jnp.dot(inverse, partial_value, precision=HIGHEST, preferred_element_type...  17.3 us
    dot_general x1, matrix products, on_device(): lax.dot_general(flat_rows, projected.reshape(-1, out_part), (((0,), (0,))...  17.1 us
    dot_general x1, matrix products, on_device(): lax.dot_general(flat_rows, flat_rows, (((0,), (0,)), ((), ())), preferred...  10.7 us
    all_to_all x1, starting transfers between devices, on_device(): lax.all_to_all(outgoing, 'expert', split_axis=1, concat_axis=1, tiled=True)  7.28 us
  transfers between devices with their start and end apart: 4, of which 3 were waited for; matrix products, arithmetic and copies ran while one was open for 10% of the time, Pallas kernels for 24%

profile of v1, /device:TPU:0, one launch (start us, length us, event | category | flops | bytes accessed | tf_op | source)
XLA Modules:
  0.0 331.9 jit_solution(2599181358682742546)
XLA Ops:
  6.5 0.0 copy-start
  6.5 0.9 fusion.13
  7.4 0.7 broadcast_multiply_fusion
  8.1 0.8 copy.23
  8.9 0.1 eq.33
  8.9 0.5 fusion.12
  9.5 0.1 select_reduce_fusion
  9.6 0.0 copy-done
  9.6 1.8 fusion.6
  11.4 2.2 copy.24
  13.5 7.3 %all-to-all-start = ((bf16[3,768,256]{2,0,1:T(4,128)(2,1)}), bf16[3,768,256]{2,0,1:T(4,128)(2,1)S(1)}, u32[]{:S(2)}, u32[]{:S(2)}) async-start(bf16[3,768,256]{2,0,1:T(4,128)(2,1)} %copy.24), calls=%async_computation | async-start | bytes 3145728 | tf_op jit(solution)/shard_map/all_to_all | solution.py:179
  20.8 4.3 %copy.27 = bf16[2,8,128,896]{3,2,0,1:T(8,128)(2,1)} copy(bf16[2,8,128,896]{3,2,1,0:T(8,128)(2,1)} %bitcast.46) | data formatting | bytes 7340032 | tf_op jit(solution)/shard_map/reshape | solution.py:160
  25.1 32.7 %all-to-all-done = bf16[3,768,256]{2,0,1:T(4,128)(2,1)S(1)} async-done(((bf16[3,768,256]{2,0,1:T(4,128)(2,1)}), bf16[3,768,256]{2,0,1:T(4,128)(2,1)S(1)}, u32[]{:S(2)}, u32[]{:S(2)}) %all-to-all-start) | async-done | bytes 1179680 | tf_op jit(solution)/shard_map/all_to_all | solution.py:179
  57.8 4.5 %all-to-all-start.1 = ((bf16[2,8,128,896]{3,2,0,1:T(8,128)(2,1)}), bf16[2,8,128,896]{3,2,0,1:T(8,128)(2,1)}, u32[]{:S(2)}, u32[]{:S(2)}) async-start(bf16[2,8,128,896]{3,2,0,1:T(8,128)(2,1)} %copy.27), calls=%async_computation.1 | async-start | bytes 7340032 | tf_op jit(solution)/shard_map/all_to_all | solution.py:161
  62.3 0.0 all-gather.2.cloned.1.call-start
  62.4 1.2 copy.25
  63.6 0.0 all-gather.2.cloned.1.call-update
  63.6 0.1 select_reduce_fusion.1
  63.7 80.0 %all-to-all-done.1 = bf16[2,8,128,896]{3,2,0,1:T(8,128)(2,1)} async-done(((bf16[2,8,128,896]{3,2,0,1:T(8,128)(2,1)}), bf16[2,8,128,896]{3,2,0,1:T(8,128)(2,1)}, u32[]{:S(2)}, u32[]{:S(2)}) %all-to-all-start.1) | async-done | bytes 3670048 | tf_op jit(solution)/shard_map/all_to_all | solution.py:161
  143.7 4.3 %copy.28 = bf16[2,8,128,896]{3,2,1,0:T(8,128)(2,1)} copy(bf16[2,8,128,896]{3,2,0,1:T(8,128)(2,1)} %all-to-all-done.1) | data formatting | bytes 7340032 | tf_op jit(solution)/shard_map/all_to_all | solution.py:161
  148.0 5.9 %gather_fusion = bf16[24,128,896]{2,1,0:T(8,128)(2,1)} fusion(bf16[16,128,896]{2,1,0:T(8,128)(2,1)} %bitcast.43, s32[1024]{0:T(1024)S(1)} %pad_clamp_fusion), kind=kCustom, calls=%fused_computation | custom fusion | bytes 11010144 | tf_op jit(solution)/shard_map/gather | solution.py:185
  154.0 5.7 %copy.29 = bf16[3,8,128,896]{3,2,0,1:T(8,128)(2,1)} copy(bf16[3,8,128,896]{3,2,1,0:T(8,128)(2,1)} %bitcast.44) | data formatting | bytes 11010048 | tf_op jit(solution)/shard_map/reshape | solution.py:187
  159.6 4.9 %all-to-all-start.2 = ((bf16[3,8,128,896]{3,2,0,1:T(8,128)(2,1)}), bf16[3,8,128,896]{3,2,0,1:T(8,128)(2,1)}, u32[]{:S(2)}, u32[]{:S(2)}) async-start(bf16[3,8,128,896]{3,2,0,1:T(8,128)(2,1)} %copy.29), calls=%async_computation.2 | async-start | bytes 11010048 | tf_op jit(solution)/shard_map/all_to_all | solution.py:188
  164.5 0.0 all-gather.2.cloned.1.call-done
  164.5 10.7 %fusion.2 = (f32[]{:T(128)}, f32[1024,1024,1]{1,0,2:T(8,128)}) fusion(bf16[3,768,1024]{2,1,0:T(8,128)(2,1)} %all-gather.2.cloned.1.call-done), kind=kOutput, calls=%fused_computation.6 | convolution fusion | flops 4834983936 | bytes 8912900 | tf_op jit(solution)/shard_map/dot_general | solution.py:192
  175.8 2.6 bitcast_add_fusion.a_ref
  178.4 79.4 %shard_map.46 = f32[1024,1024]{1,0:T(8,128)S(1)} custom-call(f32[1024,1024]{1,0:T(8,128)S(1)} %bitcast_add_fusion.a_ref), custom_call_target="tpu_custom_call" | custom-call | flops 53687091200 | bytes 8388608 | tf_op jit(solution)/shard_map/pallas_call | solution.py:132
  257.8 0.0 copy-start.1
  257.8 2.0 copy-done.1
  259.8 25.1 %all-to-all-done.2 = bf16[3,8,128,896]{3,2,0,1:T(8,128)(2,1)} async-done(((bf16[3,8,128,896]{3,2,0,1:T(8,128)(2,1)}), bf16[3,8,128,896]{3,2,0,1:T(8,128)(2,1)}, u32[]{:S(2)}, u32[]{:S(2)}) %all-to-all-start.2) | async-done | bytes 5505056 | tf_op jit(solution)/shard_map/all_to_all | solution.py:188
  284.9 5.7 %copy.30 = bf16[3,8,128,896]{3,2,1,0:T(8,128)(2,1)} copy(bf16[3,8,128,896]{3,2,0,1:T(8,128)(2,1)} %all-to-all-done.2) | data formatting | bytes 11010048 | tf_op jit(solution)/shard_map/all_to_all | solution.py:188
  290.6 17.1 %fusion.4 = f32[1024,896,1]{1,0,2:T(8,128)} fusion(bf16[3,768,1024]{2,1,0:T(8,128)(2,1)} %all-gather.2.cloned.1.call-done, bf16[3,1024,896]{2,1,0:T(8,128)(2,1)} %bitcast.45), kind=kOutput, calls=%fused_computation.10 | convolution fusion | flops 8457781248 | bytes 13893632 | tf_op jit(solution)/shard_map/dot_general | solution.py:201
  307.7 17.3 %convert_bitcast_fusion = bf16[1,1024,896]{2,1,0:T(8,128)(2,1)} fusion(f32[1024,1024]{1,0:T(8,128)} %copy-done.1, f32[1024,896,1]{1,0,2:T(8,128)} %fusion.4), kind=kOutput, calls=%fused_computation.15 | convolution fusion | flops 11275206656 | bytes 9699328 | tf_op jit(solution)/shard_map/dot_general | solution.py:207
  (3 shorter events, 0.0 us)
Async XLA Ops:
  6.5 3.0 copy-start
  13.5 44.3 %all-to-all-start = ((bf16[3,768,256]{2,0,1:T(4,128)(2,1)}), bf16[3,768,256]{2,0,1:T(4,128)(2,1)S(1)}, u32[]{:S(2)}, u32[]{:S(2)}) async-start(bf16[3,768,256]{2,0,1:T(4,128)(2,1)} %copy.24), calls=%async_computation | async-start | bytes 3145728 | tf_op jit(solution)/shard_map/all_to_all | solution.py:179
  57.8 85.9 %all-to-all-start.1 = ((bf16[2,8,128,896]{3,2,0,1:T(8,128)(2,1)}), bf16[2,8,128,896]{3,2,0,1:T(8,128)(2,1)}, u32[]{:S(2)}, u32[]{:S(2)}) async-start(bf16[2,8,128,896]{3,2,0,1:T(8,128)(2,1)} %copy.27), calls=%async_computation.1 | async-start | bytes 7340032 | tf_op jit(solution)/shard_map/all_to_all | solution.py:161
  62.3 102.2 %all-gather.2.cloned.1.call-start = ((), (), s32[]{:S(2)}) async-start(), calls=%async_computation.3 | async-start | bytes 5898240 | tf_op jit(solution)/shard_map/all_gather | solution.py:180
  159.6 125.3 %all-to-all-start.2 = ((bf16[3,8,128,896]{3,2,0,1:T(8,128)(2,1)}), bf16[3,8,128,896]{3,2,0,1:T(8,128)(2,1)}, u32[]{:S(2)}, u32[]{:S(2)}) async-start(bf16[3,8,128,896]{3,2,0,1:T(8,128)(2,1)} %copy.29), calls=%async_computation.2 | async-start | bytes 11010048 | tf_op jit(solution)/shard_map/all_to_all | solution.py:188
  257.8 2.0 copy-start.1
Sparse Core Ops, SparseCore 0:
  64.7 39.3 all-gather.1

commit v2 on v1

--- a/solution.py
+++ b/solution.py
@@ -145,6 +145,98 @@
     )(system)
 
 
+def exchange_kernel(outgoing, weights, rows, pieces, sems_row, sems_weight, sems_gather, sems_own):
+    me, ranks = lax.axis_index("expert"), lax.axis_size("expert")
+    part, parts = lax.axis_index("mp"), lax.axis_size("mp")
+    width = outgoing.shape[-1]
+    piece_rows = pieces.shape[2]
+    barrier = pltpu.get_barrier_semaphore()
+    for hop in range(1, ranks):
+        pl.semaphore_signal(barrier, inc=1, device_id={"expert": lax.rem(me + hop, ranks)})
+    for hop in range(1, parts):
+        pl.semaphore_signal(barrier, inc=1, device_id={"mp": lax.rem(part + hop, parts)})
+    pl.semaphore_wait(barrier, ranks + parts - 2)
+
+    mine = pl.ds(pl.multiple_of(part * width, width), width)
+
+    def weight_rows(owner):
+        return weights.at[:, pl.ds(pl.multiple_of(owner * piece_rows, piece_rows), piece_rows), :]
+
+    row_copies, weight_copies, gather_copies = [], [], []
+    for hop in range(1, ranks):
+        peer = lax.rem(me + hop, ranks)
+        row_copies.append(
+            pltpu.make_async_remote_copy(
+                src_ref=outgoing.at[peer],
+                dst_ref=rows.at[:, me, :, mine],
+                send_sem=sems_row.at[0, hop],
+                recv_sem=sems_row.at[1, hop],
+                device_id={"expert": peer},
+            )
+        )
+        weight_copies.append(
+            pltpu.make_async_remote_copy(
+                src_ref=weight_rows(peer),
+                dst_ref=pieces.at[me],
+                send_sem=sems_weight.at[0, hop],
+                recv_sem=sems_weight.at[1, hop],
+                device_id={"expert": peer},
+            )
+        )
+    own_rows = pltpu.make_async_copy(outgoing.at[me], rows.at[:, me, :, mine], sems_own.at[0])
+    own_weights = pltpu.make_async_copy(weight_rows(me), pieces.at[me], sems_own.at[1])
+    own_rows.start()
+    for copy in row_copies:
+        copy.start()
+    for copy in weight_copies:
+        copy.start()
+    own_weights.start()
+    own_rows.wait()
+    for copy in row_copies:
+        copy.wait()
+    for hop in range(1, parts):
+        gather_copies.append(
+            pltpu.make_async_remote_copy(
+                src_ref=rows.at[:, :, :, mine],
+                dst_ref=rows.at[:, :, :, mine],
+                send_sem=sems_gather.at[0, hop],
+                recv_sem=sems_gather.at[1, hop],
+                device_id={"mp": lax.rem(part + hop, parts)},
+            )
+        )
+    for copy in gather_copies:
+        copy.start()
+    own_weights.wait()
+    for copy in weight_copies:
+        copy.wait()
+    for copy in gather_copies:
+        copy.wait()
+
+
+def exchange(outgoing, weights, ranks, parts):
+    _, members, cap, width = outgoing.shape
+    local_count, full_width, out_part = weights.shape
+    anywhere = pl.BlockSpec(memory_space=pl.ANY)
+    return pl.pallas_call(
+        exchange_kernel,
+        out_shape=(
+            jax.ShapeDtypeStruct((members, ranks, cap, width * parts), outgoing.dtype),
+            jax.ShapeDtypeStruct(
+                (ranks, local_count, full_width // ranks, out_part), weights.dtype
+            ),
+        ),
+        in_specs=[anywhere, anywhere],
+        out_specs=(anywhere, anywhere),
+        scratch_shapes=[
+            pltpu.SemaphoreType.DMA((2, ranks)),
+            pltpu.SemaphoreType.DMA((2, ranks)),
+            pltpu.SemaphoreType.DMA((2, parts)),
+            pltpu.SemaphoreType.DMA((2,)),
+        ],
+        compiler_params=pltpu.CompilerParams(collective_id=0, has_side_effects=True),
+    )(outgoing, weights)
+
+
 def on_device(routes, routed_hidden, down_proj, merge_group):
     expert_count = lax.axis_size("expert")
     local_count = down_proj.shape[0]
@@ -157,12 +249,9 @@
     row_count = tok_count * top_count
     piece_rows = full_width // expert_count
 
-    weight_pieces = down_proj.reshape(local_count, expert_count, piece_rows, out_part)
-    weights_all = lax.all_to_all(weight_pieces, "expert", split_axis=1, concat_axis=1, tiled=True)
-
     experts = jnp.arange(expert_total, dtype=jnp.int32)
     member_rank = slot_rank(merge_group, expert_count)
-    first_slot = (member_rank * expert_count + merge_group) * slot_cap
+    first_slot = (merge_group * GMAX + member_rank) * slot_cap
     targets = routes.reshape(row_count)
     position = slot_rank(targets, expert_total)
     slot_index = position + jnp.sum(
@@ -175,18 +264,17 @@
         routed_hidden.reshape(row_count, hidden_part),
         preferred_element_type=jnp.float32,
     ).astype(jnp.bfloat16)
-    outgoing = outgoing.reshape(GMAX, expert_count * slot_cap, hidden_part)
-    arrived = lax.all_to_all(outgoing, "expert", split_axis=1, concat_axis=1, tiled=True)
-    rows = lax.all_gather(arrived, "mp", axis=2, tiled=True)
+    outgoing = outgoing.reshape(expert_count, GMAX, slot_cap, hidden_part)
+    rows, pieces = exchange(outgoing, down_proj, expert_count, lax.axis_size("mp"))
+    rows = rows.reshape(GMAX, expert_count * slot_cap, full_width)
 
     table = jnp.arange(GMAX * expert_count, dtype=jnp.int32)
-    place = member_rank * expert_count + merge_group
+    place = merge_group * GMAX + member_rank
     members = jnp.sum(jnp.where(table[:, None] == place[None, :], experts[None, :], 0), axis=1)
-    picked = weights_all.reshape(expert_total, piece_rows, out_part)[
-        (members % local_count) * expert_count + members // local_count
-    ].reshape(GMAX, expert_count, piece_rows, out_part)
-    weights_mine = lax.all_to_all(picked, "expert", split_axis=1, concat_axis=1, tiled=True)
-    member_weights = weights_mine.reshape(GMAX, full_width, out_part)
+    picked = pieces.reshape(expert_total, piece_rows, out_part)[members]
+    picked = picked.reshape(expert_count, GMAX, piece_rows, out_part)
+    arrived = lax.all_to_all(picked, "expert", split_axis=0, concat_axis=0, tiled=True)
+    member_weights = arrived.transpose(1, 0, 2, 3).reshape(GMAX, full_width, out_part)
 
     flat_rows = rows.reshape(-1, full_width)
     gram_sum = lax.dot_general(

time: 332 us -> 292 us (0.88)
  waiting for transfers between devices: 138 us -> 27.1 us
  Pallas kernels: 79.4 us -> 164 us
  starting transfers between devices: 16.7 us -> 41.1 us
  local copies, waits for them, and re-layouts: 32 us -> 12.1 us
  between operations: 14.1 us -> 0.79 us
  matrix products: 48.3 us -> 42.7 us
    all_to_all x3 -> x1, waiting for transfers between devices: 138 us -> 27.1 us  [on_device(): lax.all_to_all(picked, 'expert', split_axis=0, concat_axis=0, tiled=True)]
    pallas_call x0 -> x1, Pallas kernels: none -> 84.7 us  [exchange(): pl.pallas_call(exchange_kernel, out_shape=(jax.ShapeDtypeStruct((members,...]
    all_to_all x3 -> x1, starting transfers between devices: 16.6 us -> 41.1 us  [on_device(): lax.all_to_all(picked, 'expert', split_axis=0, concat_axis=0, tiled=True)]
    reshape x3 -> x0, local copies, waits for them, and re-layouts: 12.1 us -> none  [the longest x1 5.67 us: on_device(): picked = weights_all.reshape(expert_total, piece_rows, out_part)[members...]
    dot_general x1, matrix products: 17.1 us -> 5.25 us  [on_device(): lax.dot_general(flat_rows, projected.reshape(-1, out_part), (((0,), (0,))...]
    all_to_all x3 -> x0, local copies, waits for them, and re-layouts: 11.2 us -> none  [the longest x1 5.67 us: on_device(): lax.all_to_all(picked, 'expert', split_axis=1, concat_axis=1, tiled=True)]
    dot_general x0 -> x1, matrix products: none -> 7.9 us  [on_device(): jnp.einsum('rsf,rfd->rsd', rows, member_weights, preferred_element_type=j...]
  transfers between devices with their start and end apart: 4 -> 1, of which waited for: 3 -> 1; matrix products, arithmetic and copies ran while one was open for 10% -> 5% of each run, Pallas kernels for 24% -> 27%
where the time goes in v2:
time: 292 us; the launch traced here: 291 us
  Pallas kernels  164 us (56%)
  matrix products  42.7 us (15%)
  starting transfers between devices  41.1 us (14%)
  waiting for transfers between devices  27.1 us (9%)
  local copies, waits for them, and re-layouts  12.1 us (4%)
  other arithmetic  3.42 us (1%)
    pallas_call x1, Pallas kernels, exchange(): pl.pallas_call(exchange_kernel, out_shape=(jax.ShapeDtypeStruct((members,...  84.7 us
    pallas_call x1, Pallas kernels, spd_inverse(): pl.pallas_call(inverse_kernel, out_shape=jax.ShapeDtypeStruct(system.shap...  79.2 us
    all_to_all x1, starting transfers between devices, on_device(): lax.all_to_all(picked, 'expert', split_axis=0, concat_axis=0, tiled=True)  41.1 us
    all_to_all x1, waiting for transfers between devices, on_device(): lax.all_to_all(picked, 'expert', split_axis=0, concat_axis=0, tiled=True)  27.1 us
    dot_general x1, matrix products, on_device(): jnp.dot(inverse, partial_value, precision=HIGHEST, preferred_element_type...  14.7 us
    dot_general x1, matrix products, on_device(): lax.dot_general(flat_rows, flat_rows, (((0,), (0,)), ((), ())), preferred...  10.7 us
    dot_general x1, matrix products, on_device(): jnp.einsum('rsf,rfd->rsd', rows, member_weights, preferred_element_type=j...  7.9 us
    gather x1, local copies, waits for them, and re-layouts, on_device(): picked = pieces.reshape(expert_total, piece_rows, out_part)[members]  5.93 us
  transfers between devices with their start and end apart: 1, of which 1 were waited for; matrix products, arithmetic and copies ran while one was open for 5% of the time, Pallas kernels for 27%

profile of v2, /device:TPU:0, one launch (start us, length us, event | category | flops | bytes accessed | tf_op | source)
XLA Modules:
  0.0 291.1 jit_solution(18213723431638320207)
XLA Ops:
  0.0 0.0 copy-start
  0.0 0.9 fusion.7
  0.9 0.7 broadcast_multiply_fusion
  1.5 0.1 select_reduce_fusion.1
  1.6 0.8 copy.10
  2.4 0.1 eq.32
  2.5 0.5 fusion.6
  3.0 0.1 select_reduce_fusion
  3.1 0.0 copy-done
  3.1 2.8 fusion.4
  6.0 84.7 %shard_map.46 = (bf16[3,8,96,1024]{3,2,1,0:T(8,128)(2,1)}, bf16[8,2,128,896]{3,2,1,0:T(8,128)(2,1)}) custom-call(bf16[8,3,96,256]{3,2,1,0:T(8,128)(2,1)} %bitcast.35, bf16[2,1024,896]{2,1,0:T(8,128)(2,1)} %weights.1), custom_call_target="tpu_custom_call" | custom-call | tf_op jit(solution)/shard_map/pallas_call | solution.py:220
  90.7 5.9 %gather_fusion = bf16[24,128,896]{2,1,0:T(8,128)(2,1)} fusion(bf16[16,128,896]{2,1,0:T(8,128)(2,1)} %bitcast.33, s32[1024]{0:T(1024)S(1)} %pad_clamp_fusion), kind=kCustom, calls=%fused_computation | custom fusion | bytes 11010144 | tf_op jit(solution)/shard_map/gather | solution.py:274
  96.7 41.1 %all-to-all-start = ((bf16[8,3,128,896]{3,2,1,0:T(8,128)(2,1)}), bf16[8,3,128,896]{3,2,1,0:T(8,128)(2,1)}, u32[]{:S(2)}, u32[]{:S(2)}) async-start(bf16[8,3,128,896]{3,2,1,0:T(8,128)(2,1)} %bitcast.32), calls=%async_computation | async-start | bytes 11010048 | tf_op jit(solution)/shard_map/all_to_all | solution.py:276
  137.8 10.7 %fusion.2 = (f32[]{:T(128)}, f32[1024,1024,1,1]{1,0,3,2:T(8,128)}) fusion(bf16[3,8,96,1024]{3,2,1,0:T(8,128)(2,1)} %get-tuple-element.7), kind=kOutput, calls=%fused_computation.6 | convolution fusion | flops 4834983936 | bytes 8912900 | tf_op jit(solution)/shard_map/dot_general | solution.py:280
  149.1 2.6 bitcast_add_fusion.a_ref
  151.6 79.2 %shard_map.47 = f32[1024,1024]{1,0:T(8,128)S(1)} custom-call(f32[1024,1024]{1,0:T(8,128)S(1)} %bitcast_add_fusion.a_ref), custom_call_target="tpu_custom_call" | custom-call | flops 53687091200 | bytes 8388608 | tf_op jit(solution)/shard_map/pallas_call | solution.py:132
  230.8 0.0 copy-start.1
  230.8 2.0 copy-done.1
  232.8 27.1 %all-to-all-done = bf16[8,3,128,896]{3,2,1,0:T(8,128)(2,1)} async-done(((bf16[8,3,128,896]{3,2,1,0:T(8,128)(2,1)}), bf16[8,3,128,896]{3,2,1,0:T(8,128)(2,1)}, u32[]{:S(2)}, u32[]{:S(2)}) %all-to-all-start) | async-done | bytes 5505056 | tf_op jit(solution)/shard_map/all_to_all | solution.py:276
  259.9 0.0 slice-start
  259.9 3.3 %copy.11 = bf16[3,8,128,896]{3,2,1,0:T(8,128)(2,1)S(1)} copy(bf16[3,8,128,896]{3,2,0,1:T(8,128)(2,1)} %bitcast.11) | data formatting | bytes 11010048 | tf_op jit(solution)/shard_map/transpose | solution.py:277
  263.2 0.0 slice-start.1
  263.2 7.9 %convolution_convert_fusion = bf16[3,768,896]{2,1,0:T(8,128)(2,1)S(1)} fusion(bf16[3,768,1024]{2,1,0:T(8,128)(2,1)} %bitcast.36, bf16[3,1024,896]{2,1,0:T(8,128)(2,1)S(1)} %bitcast.34), kind=kOutput, calls=%fused_computation.11 | convolution fusion | flops 4229922816 | bytes 14352384 | tf_op jit(solution)/shard_map/rsf,rfd->rsd/dot_general | solution.py:286
  271.1 0.0 slice-done
  271.1 0.0 slice-done.1
  271.1 0.0 copy-start.2
  271.1 5.3 %fusion.12 = f32[1024,896]{1,0:T(8,128)S(1)} fusion(bf16[2304,1024]{1,0:T(8,128)(2,1)S(1)} %bitcast.39, bf16[2304,896]{1,0:T(8,128)(2,1)S(1)} %bitcast.40), kind=kOutput, calls=%fused_computation.32 | convolution fusion | flops 4227858432 | bytes 12517376 | tf_op jit(solution)/shard_map/dot_general | solution.py:289
  276.4 0.0 copy-done.2
  276.4 14.7 %convert_bitcast_fusion = bf16[1,1024,896]{2,1,0:T(8,128)(2,1)} fusion(f32[1024,1024]{1,0:T(8,128)S(1)} %copy-done.2, f32[1024,896]{1,0:T(8,128)S(1)} %fusion.12), kind=kOutput, calls=%fused_computation.12 | convolution fusion | flops 11275206656 | bytes 9699328 | tf_op jit(solution)/shard_map/dot_general | solution.py:295
  (4 shorter events, 0.0 us)
Async XLA Ops:
  0.0 3.1 %copy-start = (bf16[128,8,256]{2,1,0:T(8,128)(2,1)S(1)}, bf16[128,8,256]{2,1,0:T(8,128)(2,1)}, u32[]{:S(2)}) copy-start(bf16[128,8,256]{2,1,0:T(8,128)(2,1)} %param.5) | copy-start | bytes 1572868
  96.7 163.2 %all-to-all-start = ((bf16[8,3,128,896]{3,2,1,0:T(8,128)(2,1)}), bf16[8,3,128,896]{3,2,1,0:T(8,128)(2,1)}, u32[]{:S(2)}, u32[]{:S(2)}) async-start(bf16[8,3,128,896]{3,2,1,0:T(8,128)(2,1)} %bitcast.32), calls=%async_computation | async-start | bytes 11010048 | tf_op jit(solution)/shard_map/all_to_all | solution.py:276
  230.8 2.0 copy-start.1
  259.9 11.2 %slice-start = ((s8[4718592]{0:T(1024)(128)(4,1)}), s8[4194304]{0:T(1024)(128)(4,1)S(1)}, s32[]{:S(2)}) async-start(s8[4718592]{0:T(1024)(128)(4,1)} %bitcast.37), calls=%async_computation.1 | async-start | bytes 8388608
  263.2 7.9 %slice-start.1 = ((s8[4718592]{0:T(1024)(128)(4,1)}), s8[524288]{0:T(1024)(128)(4,1)S(1)}, s32[]{:S(2)}) async-start(s8[4718592]{0:T(1024)(128)(4,1)} %bitcast.37), calls=%async_computation.2 | async-start | bytes 1048576
  271.1 5.3 %copy-start.2 = (f32[1024,1024]{1,0:T(8,128)S(1)}, f32[1024,1024]{1,0:T(8,128)}, u32[]{:S(2)}) copy-start(f32[1024,1024]{1,0:T(8,128)} %copy-done.1) | copy-start | bytes 12582916

commit v3 on v2

--- a/solution.py
+++ b/solution.py
@@ -293,7 +293,7 @@
         preferred_element_type=jnp.float32,
     )
     merged = jnp.dot(
-        inverse, partial_value, precision=HIGHEST, preferred_element_type=jnp.float32
+        inverse, partial_value, precision=lax.Precision.HIGH, preferred_element_type=jnp.float32
     )
     return merged.astype(jnp.bfloat16).reshape(1, full_width, out_part)
 

time: 292 us -> 285 us (0.976)
  matrix products: 42.7 us -> 36 us
    dot_general x1, matrix products: 14.7 us -> 7.97 us  [on_device(): jnp.dot(inverse, partial_value, precision=lax.Precision.HIGH, preferred_e...]
  transfers between devices with their start and end apart: 1 -> 1, of which waited for: 1 -> 1; matrix products, arithmetic and copies ran while one was open for 5% -> 5% of each run, Pallas kernels for 27% -> 28%
where the time goes in v3:
time: 285 us; the launch traced here: 284 us
  Pallas kernels  164 us (58%)
  starting transfers between devices  41.1 us (14%)
  matrix products  36 us (13%)
  waiting for transfers between devices  27.1 us (10%)
  local copies, waits for them, and re-layouts  12.1 us (4%)
  other arithmetic  3.42 us (1%)
    pallas_call x1, Pallas kernels, exchange(): pl.pallas_call(exchange_kernel, out_shape=(jax.ShapeDtypeStruct((members,...  84.7 us
    pallas_call x1, Pallas kernels, spd_inverse(): pl.pallas_call(inverse_kernel, out_shape=jax.ShapeDtypeStruct(system.shap...  79.2 us
    all_to_all x1, starting transfers between devices, on_device(): lax.all_to_all(picked, 'expert', split_axis=0, concat_axis=0, tiled=True)  41.1 us
    all_to_all x1, waiting for transfers between devices, on_device(): lax.all_to_all(picked, 'expert', split_axis=0, concat_axis=0, tiled=True)  27.1 us
    dot_general x1, matrix products, on_device(): lax.dot_general(flat_rows, flat_rows, (((0,), (0,)), ((), ())), preferred...  10.7 us
    dot_general x1, matrix products, on_device(): jnp.dot(inverse, partial_value, precision=lax.Precision.HIGH, preferred_e...  7.97 us
    dot_general x1, matrix products, on_device(): jnp.einsum('rsf,rfd->rsd', rows, member_weights, preferred_element_type=j...  7.9 us
    gather x1, local copies, waits for them, and re-layouts, on_device(): picked = pieces.reshape(expert_total, piece_rows, out_part)[members]  5.93 us
  transfers between devices with their start and end apart: 1, of which 1 were waited for; matrix products, arithmetic and copies ran while one was open for 5% of the time, Pallas kernels for 28%

profile of v3, /device:TPU:0, one launch (start us, length us, event | category | flops | bytes accessed | tf_op | source)
XLA Modules:
  0.0 284.4 jit_solution(7396237111106219360)
XLA Ops:
  0.0 0.0 copy-start
  0.0 0.9 fusion.7
  0.9 0.7 broadcast_multiply_fusion
  1.5 0.1 select_reduce_fusion.1
  1.6 0.8 copy.10
  2.4 0.1 eq.32
  2.5 0.5 fusion.6
  3.0 0.1 select_reduce_fusion
  3.1 0.0 copy-done
  3.1 2.8 fusion.4
  6.0 84.7 %shard_map.46 = (bf16[3,8,96,1024]{3,2,1,0:T(8,128)(2,1)}, bf16[8,2,128,896]{3,2,1,0:T(8,128)(2,1)}) custom-call(bf16[8,3,96,256]{3,2,1,0:T(8,128)(2,1)} %bitcast.35, bf16[2,1024,896]{2,1,0:T(8,128)(2,1)} %weights.1), custom_call_target="tpu_custom_call" | custom-call | tf_op jit(solution)/shard_map/pallas_call | solution.py:220
  90.7 5.9 %gather_fusion = bf16[24,128,896]{2,1,0:T(8,128)(2,1)} fusion(bf16[16,128,896]{2,1,0:T(8,128)(2,1)} %bitcast.33, s32[1024]{0:T(1024)S(1)} %pad_clamp_fusion), kind=kCustom, calls=%fused_computation | custom fusion | bytes 11010144 | tf_op jit(solution)/shard_map/gather | solution.py:274
  96.7 41.1 %all-to-all-start = ((bf16[8,3,128,896]{3,2,1,0:T(8,128)(2,1)}), bf16[8,3,128,896]{3,2,1,0:T(8,128)(2,1)}, u32[]{:S(2)}, u32[]{:S(2)}) async-start(bf16[8,3,128,896]{3,2,1,0:T(8,128)(2,1)} %bitcast.32), calls=%async_computation | async-start | bytes 11010048 | tf_op jit(solution)/shard_map/all_to_all | solution.py:276
  137.8 10.7 %fusion.2 = (f32[]{:T(128)}, f32[1024,1024,1,1]{1,0,3,2:T(8,128)}) fusion(bf16[3,8,96,1024]{3,2,1,0:T(8,128)(2,1)} %get-tuple-element.7), kind=kOutput, calls=%fused_computation.6 | convolution fusion | flops 4834983936 | bytes 8912900 | tf_op jit(solution)/shard_map/dot_general | solution.py:280
  149.1 2.6 bitcast_add_fusion.a_ref
  151.6 79.2 %shard_map.47 = f32[1024,1024]{1,0:T(8,128)S(1)} custom-call(f32[1024,1024]{1,0:T(8,128)S(1)} %bitcast_add_fusion.a_ref), custom_call_target="tpu_custom_call" | custom-call | flops 53687091200 | bytes 8388608 | tf_op jit(solution)/shard_map/pallas_call | solution.py:132
  230.8 0.0 copy-start.1
  230.8 2.0 copy-done.1
  232.8 27.1 %all-to-all-done = bf16[8,3,128,896]{3,2,1,0:T(8,128)(2,1)} async-done(((bf16[8,3,128,896]{3,2,1,0:T(8,128)(2,1)}), bf16[8,3,128,896]{3,2,1,0:T(8,128)(2,1)}, u32[]{:S(2)}, u32[]{:S(2)}) %all-to-all-start) | async-done | bytes 5505056 | tf_op jit(solution)/shard_map/all_to_all | solution.py:276
  259.9 0.0 slice-start
  259.9 3.3 %copy.11 = bf16[3,8,128,896]{3,2,1,0:T(8,128)(2,1)S(1)} copy(bf16[3,8,128,896]{3,2,0,1:T(8,128)(2,1)} %bitcast.11) | data formatting | bytes 11010048 | tf_op jit(solution)/shard_map/transpose | solution.py:277
  263.2 0.0 slice-start.1
  263.2 7.9 %convolution_convert_fusion = bf16[3,768,896]{2,1,0:T(8,128)(2,1)S(1)} fusion(bf16[3,768,1024]{2,1,0:T(8,128)(2,1)} %bitcast.36, bf16[3,1024,896]{2,1,0:T(8,128)(2,1)S(1)} %bitcast.34), kind=kOutput, calls=%fused_computation.11 | convolution fusion | flops 4229922816 | bytes 14352384 | tf_op jit(solution)/shard_map/rsf,rfd->rsd/dot_general | solution.py:286
  271.1 0.0 slice-done
  271.1 0.0 slice-done.1
  271.1 0.0 copy-start.2
  271.1 5.3 %fusion.12 = f32[1024,896]{1,0:T(8,128)S(1)} fusion(bf16[2304,1024]{1,0:T(8,128)(2,1)S(1)} %bitcast.39, bf16[2304,896]{1,0:T(8,128)(2,1)S(1)} %bitcast.40), kind=kOutput, calls=%fused_computation.32 | convolution fusion | flops 4227858432 | bytes 12517376 | tf_op jit(solution)/shard_map/dot_general | solution.py:289
  276.4 0.0 copy-done.2
  276.4 8.0 %convert_bitcast_fusion = bf16[1,1024,896]{2,1,0:T(8,128)(2,1)} fusion(f32[1024,1024]{1,0:T(8,128)S(1)} %copy-done.2, f32[1024,896]{1,0:T(8,128)S(1)} %fusion.12), kind=kOutput, calls=%fused_computation.12 | convolution fusion | flops 5638062080 | bytes 9699328 | tf_op jit(solution)/shard_map/dot_general | solution.py:295
  (4 shorter events, 0.0 us)
Async XLA Ops:
  0.0 3.1 %copy-start = (bf16[128,8,256]{2,1,0:T(8,128)(2,1)S(1)}, bf16[128,8,256]{2,1,0:T(8,128)(2,1)}, u32[]{:S(2)}) copy-start(bf16[128,8,256]{2,1,0:T(8,128)(2,1)} %param.5) | copy-start | bytes 1572868
  96.7 163.2 %all-to-all-start = ((bf16[8,3,128,896]{3,2,1,0:T(8,128)(2,1)}), bf16[8,3,128,896]{3,2,1,0:T(8,128)(2,1)}, u32[]{:S(2)}, u32[]{:S(2)}) async-start(bf16[8,3,128,896]{3,2,1,0:T(8,128)(2,1)} %bitcast.32), calls=%async_computation | async-start | bytes 11010048 | tf_op jit(solution)/shard_map/all_to_all | solution.py:276
  230.8 2.0 copy-start.1
  259.9 11.2 %slice-start = ((s8[4718592]{0:T(1024)(128)(4,1)}), s8[4194304]{0:T(1024)(128)(4,1)S(1)}, s32[]{:S(2)}) async-start(s8[4718592]{0:T(1024)(128)(4,1)} %bitcast.37), calls=%async_computation.1 | async-start | bytes 8388608
  263.2 7.9 %slice-start.1 = ((s8[4718592]{0:T(1024)(128)(4,1)}), s8[524288]{0:T(1024)(128)(4,1)S(1)}, s32[]{:S(2)}) async-start(s8[4718592]{0:T(1024)(128)(4,1)} %bitcast.37), calls=%async_computation.2 | async-start | bytes 1048576
  271.1 5.3 %copy-start.2 = (f32[1024,1024]{1,0:T(8,128)S(1)}, f32[1024,1024]{1,0:T(8,128)}, u32[]{:S(2)}) copy-start(f32[1024,1024]{1,0:T(8,128)} %copy-done.1) | copy-start | bytes 12582916
